TPU v7x, 32 devices: a whole 2x2x4 slice. The times are simulated.
32 devices in a mesh: row: 4 (over y, x), col: 8 (over z, core).
Axes of the slice: x: 2, y: 2, z: 4, core: 2. Of those that a mesh axis runs over, the one named last changes fastest.
Arguments:
- boundary_start: float32 [16384, 128], P('row'), may hold values from -6 to 6
- volume_start: float32 [256, 512, 128], P(('row', 'col')), may hold values from -6 to 6
- diag_part: float32 [16384], P(('row', 'col')), may hold values from 1 to 2
- incident: float32 [16384, 128], P(('row', 'col')), may hold values from -6 to 6
- kernel: float32 [16384, 16384], P('row', 'col'), may hold values from -0.015625 to 0.015625
- elem_mats: float32 [256, 512, 512], P(('row', 'col')), may hold values from -0.078125 to 0.078125
- trace_owner: int32 [16384, 1], replicated, may hold values from 0 to 31; in each aligned block of 512 rows (0 to 511, 512 to 1023, ...) at most 32 rows name the same one
- trace_slot: int32 [16384], replicated, may hold values from 0 to 4095
- return_owner: int32 [16384, 1], replicated, may hold values from 0 to 31; in each aligned block of 512 rows (0 to 511, 512 to 1023, ...) at most 32 rows name the same one
- return_slot: int32 [16384], replicated, may hold values from 0 to 4095
- face_match: int32 [256, 64], P(('row', 'col')), may hold values from 0 to 63, each once within a row
Outputs:
- boundary_final: float32 [16384, 128], P('row')
- volume_final: float32 [256, 512, 128], P(('row', 'col'))
Inputs may be any that keep to these rules, and one draw needn't show every extreme that they name: `trace_owner`: in each aligned block of 512 boundary rows (the rows of one device), no device is named more than 32 times; some device is named exactly 32 times in some block. `return_owner`: in each aligned block of 512 boundary rows (the rows of one device), no device is named more than 32 times; some device is named exactly 32 times in some block. `face_match`: each row is a permutation of 0 to 63.
All inputs are finite; a program needn't handle non-finite values.
Results may differ from a plain program's by a relative error of at most 0.0001.
Values sent between devices are 32-bit elements; how exact they have to be, the bound alone decides.
A program may use at most 128 MiB of HBM per device.

v0:
```python
import functools

import jax
import jax.numpy as jnp
from jax import lax
from jax.experimental import pallas as pl
from jax.experimental.pallas import tpu as pltpu
from jax.sharding import PartitionSpec as P

ITERS = 3


boundary_step = 0.5
volume_step = 0.6
face_weight = 0.5


def passed_along(block, axis, distance):
    devices = range(lax.axis_size(axis))
    route = [(i - distance, i) for i in devices if i - distance in devices]
    return lax.ppermute(block, axis, route)


def exchange_kernel(reduces, finishes, *refs):
    rows_n, cols_n = lax.axis_size("row"), lax.axis_size("col")
    pairs = cols_n // 2
    per_panel = cols_n // rows_n
    r, c = lax.axis_index("row"), lax.axis_index("col")
    z, h = c // 2, c % 2
    partner = z * 2 + (1 - h)
    target_row, target_col = c % rows_n, r * per_panel + c // rows_n
    source_row, source_col = c // per_panel, (c % per_panel) * rows_n + r
    stays = (target_row == r) & (target_col == c)

    if reduces:
        panel_wide, trace_wide, trace_take, kernel, elem_mats, volume = refs[:6]
        flux_send, flux_take, face_wide, face_match, middle, volume_out = refs[6:12]
        refs = refs[12:]
    else:
        middle, refs = refs[0], refs[1:]
    if finishes:
        out, refs = refs[0], refs[1:]
    else:
        share, out, refs = refs[0], refs[1], refs[2:]
    if reduces:
        from_pair, summed_pair, from_line, refs = refs[0], refs[1], refs[2], refs[3:]
        pair_send, pair_recv, line_send, line_recv, refs = refs[0], refs[1], refs[2], refs[3], refs[4:]
        partial, kernel_blocks, elem_blocks, kernel_sem, elem_sem = refs[:5]
        leaving, landed, flux_wide, flux_out, flux_in = refs[5:10]
        refs = refs[10:]
    if finishes:
        out_send, out_recv, back_send, back_recv = refs
    else:
        move_send, move_recv, row_send, row_recv = refs

    barrier = pltpu.get_barrier_semaphore()

    def greet(row, col):
        pl.semaphore_signal(barrier, inc=1, device_id=(row, col), device_id_type=pl.DeviceIdType.MESH)

    greeted = 0
    if reduces:
        for step in range(1, cols_n):
            greet(r, (c + step) % cols_n)
        greeted += cols_n - 1
    if not finishes:
        for step in range(1, rows_n):
            greet((r + step) % rows_n, c)
        greeted += rows_n - 1

        @pl.when(jnp.logical_not(stays))
        def _():
            greet(source_row, source_col)

        greeted += jnp.where(stays, 0, 1)

    pl.semaphore_wait(barrier, greeted)

    def remote(src, dst, send, recv, row, col):
        return pltpu.make_async_remote_copy(
            src_ref=src,
            dst_ref=dst,
            send_sem=send,
            recv_sem=recv,
            device_id=(row, col),
            device_id_type=pl.DeviceIdType.MESH,
        )

    if reduces:
        share_rows, columns = middle.shape
        tile = min(128, share_rows)
        elem_count, node_count, _ = volume.shape
        face_count = face_match.shape[1]

        def parts(block):
            high = block.astype(jnp.bfloat16)
            low = (block - high.astype(jnp.float32)).astype(jnp.bfloat16)
            return high, low

        def product(left, right):
            return jnp.dot(left, right, preferred_element_type=jnp.float32)

        def one_hot(hits):
            return jnp.where(hits, 1.0, 0.0).astype(jnp.bfloat16)

        def product_block(block, slot):
            def step(t, carry):
                rows = pl.ds(pl.multiple_of(t * tile, tile), tile)
                high, low = parts(kernel_blocks[slot, rows, :])
                place = lax.broadcasted_iota(jnp.int32, (tile, trace_wide.shape[1]), 0) + t * tile
                wide = product(high, panel_wide[...]) + product(low, panel_wide[...])
                wide -= product(one_hot(place == trace_take[block]), trace_wide[block])
                partial[block, rows, :] = wide[:, :columns] + wide[:, columns:]
                return carry

            lax.fori_loop(0, share_rows // tile, step, 0)

        def volume_step_of(e, carry):
            field = volume[e]
            high, low = parts(elem_blocks[e])
            field_wide = jnp.concatenate(parts(field), axis=1)
            wide = product(high, field_wide) + product(low, field_wide)
            place = lax.broadcasted_iota(jnp.int32, (node_count, flux_wide.shape[0]), 0) + e * node_count
            wide -= product(one_hot(place == flux_take[...]), flux_wide[...])
            volume_out[e] = field - volume_step * (field + wide[:, :columns] + wide[:, columns:])
            node = lax.broadcasted_iota(jnp.int32, (face_count, face_count), 1)
            face = product(one_hot(node == face_match[e]), face_wide[e])
            matched = face[:, :columns] + face[:, columns:]
            volume_out[e, :face_count, :] += volume_step * face_weight * matched
            return carry

        elem_load = pltpu.make_async_copy(elem_mats, elem_blocks, elem_sem)
        order = []
        for step in range(1, pairs + 1):
            other = (z + step) % pairs
            order += [other * 2 + (1 - h), other * 2 + h]

        def load(i):
            return pltpu.make_async_copy(
                kernel.at[pl.ds(pl.multiple_of(order[i] * share_rows, share_rows), share_rows), :],
                kernel_blocks.at[i % 2],
                kernel_sem.at[i % 2],
            )

        load(0).start()
        elem_load.start()

        def picked(member):
            node = lax.broadcasted_iota(jnp.int32, (flux_send.shape[1], panel_wide.shape[0]), 1)
            wide = product(one_hot(node == flux_send[member]), panel_wide[...])
            return wide[:, :columns] + wide[:, columns:]

        flux_copies = []
        for step in range(1, cols_n):
            member = (c + step) % cols_n
            leaving[step - 1] = picked(member)
            copy = remote(
                leaving.at[step - 1], landed.at[c], flux_out.at[step - 1], flux_in.at[step - 1], r, member
            )
            copy.start()
            flux_copies.append(copy)
        landed[c] = picked(c)
        pair_copies = []
        line_copies = []

        def pass_on(step):
            other = (z + step) % pairs
            pair_copies[step - 1].wait_recv()
            summed_pair[step - 1] = from_pair[step - 1] + partial[other * 2 + h]
            copy = remote(
                summed_pair.at[step - 1], from_line.at[step - 1],
                line_send.at[step - 1], line_recv.at[step - 1], r, other * 2 + h,
            )
            copy.start()
            line_copies.append(copy)

        for i in range(2 * pairs):
            if i + 1 < 2 * pairs:
                load(i + 1).start()
            load(i).wait()
            product_block(order[i], i % 2)
            if i % 2 == 0:
                copy = remote(
                    partial.at[order[i]], from_pair.at[i // 2],
                    pair_send.at[i // 2], pair_recv.at[i // 2], r, partner,
                )
                copy.start()
                pair_copies.append(copy)
            elif i // 2 + 1 < pairs:
                pass_on(i // 2 + 1)
        elem_load.wait()
        for copy in flux_copies:
            copy.wait_recv()
        flux_wide[...] = jnp.concatenate(parts(landed[...].reshape(flux_wide.shape[0], columns)), axis=1)
        lax.fori_loop(0, elem_count // 2, volume_step_of, 0)
        pair_copies[pairs - 1].wait_recv()
        total = from_pair[pairs - 1] + partial[z * 2 + h]
        summed_pair[pairs - 1] = total
        for step in range(1, pairs):
            line_copies[step - 1].wait_recv()
            summed_pair[pairs - 1] += from_line[step - 1]
        fresh = middle[...] - boundary_step * summed_pair[pairs - 1]
        if finishes:
            out[c] = fresh
        else:
            share[...] = fresh
    else:
        share[...] = middle[...]

    if finishes:
        sent = []
        for step in range(1, pairs):
            copy = remote(
                out.at[c], out.at[c], out_send.at[step - 1], out_recv.at[step - 1],
                r, ((z + step) % pairs) * 2 + h,
            )
            copy.start()
            sent.append(copy)
        back = [remote(out.at[c], out.at[c], back_send.at[0], back_recv.at[0], r, partner)]
        back[0].start()
        for step in range(1, pairs):
            origin = ((z - step + pairs) % pairs) * 2 + h
            sent[step - 1].wait_recv()
            copy = remote(
                out.at[origin], out.at[origin], back_send.at[step], back_recv.at[step], r, partner
            )
            copy.start()
            back.append(copy)
        if reduces:
            lax.fori_loop(elem_count // 2, elem_count, volume_step_of, 0)
        for copy in back:
            copy.wait_recv()
        for copy in sent + back:
            copy.wait_send()
    else:
        @pl.when(stays)
        def _():
            out[r] = share[...]

        move = remote(share, out.at[target_row], move_send, move_recv, target_row, target_col)

        @pl.when(jnp.logical_not(stays))
        def _():
            move.start()
            move.wait_recv()

        sent = []
        for step in range(1, rows_n):
            copy = remote(
                out.at[r], out.at[r], row_send.at[step - 1], row_recv.at[step - 1],
                (r + step) % rows_n, c,
            )
            copy.start()
            sent.append(copy)
        if reduces:
            lax.fori_loop(elem_count // 2, elem_count, volume_step_of, 0)
        for copy in sent:
            copy.wait_recv()
        for copy in sent:
            copy.wait_send()

        @pl.when(jnp.logical_not(stays))
        def _():
            move.wait_send()

    if reduces:
        for copy in pair_copies + line_copies + flux_copies:
            copy.wait_send()


def exchange(reduces, finishes, *operands):
    rows_n, cols_n = lax.axis_size("row"), lax.axis_size("col")
    pairs = cols_n // 2
    rows, columns = operands[-1].shape
    block = (rows, columns)
    in_vmem = pl.BlockSpec(memory_space=pltpu.VMEM)
    if finishes:
        shapes = [jax.ShapeDtypeStruct((cols_n,) + block, jnp.float32)]
    else:
        shapes = [
            jax.ShapeDtypeStruct(block, jnp.float32),
            jax.ShapeDtypeStruct((rows_n,) + block, jnp.float32),
        ]
    scratch = []
    in_specs = [in_vmem] * len(operands)
    if reduces:
        kernel, elem_mats, volume = operands[3:6]
        shapes = [jax.ShapeDtypeStruct(volume.shape, jnp.float32)] + shapes
        in_specs[3] = in_specs[4] = pl.BlockSpec(memory_space=pl.ANY)
        scratch += [pltpu.VMEM((pairs,) + block, jnp.float32), pltpu.VMEM((pairs,) + block, jnp.float32)]
        scratch += [pltpu.VMEM((pairs - 1,) + block, jnp.float32)]
        scratch += [pltpu.SemaphoreType.DMA((pairs,))] * 2 + [pltpu.SemaphoreType.DMA((pairs - 1,))] * 2
        scratch += [
            pltpu.VMEM((cols_n,) + block, jnp.float32),
            pltpu.VMEM((2, rows, kernel.shape[1]), jnp.float32),
            pltpu.VMEM(elem_mats.shape, jnp.float32),
            pltpu.SemaphoreType.DMA((2,)),
            pltpu.SemaphoreType.DMA,
        ]
        slots = operands[6].shape[1]
        scratch += [
            pltpu.VMEM((cols_n - 1, slots, columns), jnp.float32),
            pltpu.VMEM((cols_n, slots, columns), jnp.float32),
            pltpu.VMEM((cols_n * slots, 2 * columns), jnp.bfloat16),
        ]
        scratch += [pltpu.SemaphoreType.DMA((cols_n - 1,))] * 2
    if finishes:
        scratch += [pltpu.SemaphoreType.DMA((pairs - 1,))] * 2 + [pltpu.SemaphoreType.DMA((pairs,))] * 2
    else:
        scratch += [pltpu.SemaphoreType.DMA] * 2 + [pltpu.SemaphoreType.DMA((rows_n - 1,))] * 2
    return pl.pallas_call(
        functools.partial(exchange_kernel, reduces, finishes),
        out_shape=shapes,
        in_specs=in_specs,
        out_specs=[in_vmem] * len(shapes),
        scratch_shapes=scratch,
        compiler_params=pltpu.CompilerParams(
            collective_id=int(reduces) + int(finishes), has_side_effects=True, vmem_limit_bytes=(48 << 20) if reduces else (8 << 20)
        ),
        cost_estimate=pl.CostEstimate(flops=1000, bytes_accessed=150_000_000, transcendentals=0),
    )(*operands)


def halves(block, axis):
    high = lax.reduce_precision(block, 8, 7)
    low = block - high
    return jnp.concatenate([high.astype(jnp.bfloat16), low.astype(jnp.bfloat16)], axis=axis)


def block_plan(owner_blocks, slot_blocks, device_self, capacity):
    mine_rows = owner_blocks == device_self
    rank_rows = jnp.cumsum(mine_rows.astype(jnp.int32), axis=1) - 1
    places = jnp.arange(capacity, dtype=jnp.int32)
    select = mine_rows[:, None, :] & (rank_rows[:, None, :] == places[None, :, None])
    index = jnp.sum(jnp.where(select, slot_blocks[:, None, :], 0), axis=2)
    valid_slot = jnp.any(select, axis=2)
    return (index, valid_slot)


def shards(
    boundary_start,
    volume_start,
    diag_part,
    incident,
    kernel,
    elem_mats,
    trace_owner,
    trace_slot,
    return_owner,
    return_slot,
    face_match,
):
    devices = lax.axis_size(("row", "col"))
    row_devices = lax.axis_size("row")
    col_devices = lax.axis_size("col")
    device_self = lax.axis_index(("row", "col"))
    row_index = lax.axis_index("row")
    col_index = lax.axis_index("col")
    total_rows = trace_slot.shape[0]
    share_rows = total_rows // devices
    capacity = max(2, 2 * share_rows // devices)
    per_panel = col_devices // row_devices
    elem_count, node_count, columns = volume_start.shape
    face_count = face_match.shape[1]
    row_panel = boundary_start.shape[0]
    positions = jnp.arange(share_rows, dtype=jnp.int32)
    trace_blocks = trace_owner[:, 0].reshape(devices, share_rows)
    trace_slots = trace_slot.reshape(devices, share_rows)
    return_blocks = return_owner[:, 0].reshape(devices, share_rows)
    return_slots = return_slot.reshape(devices, share_rows)

    trace_send, _ = block_plan(trace_blocks, trace_slots, device_self, capacity)
    own_trace = lax.dynamic_slice_in_dim(trace_blocks, row_index * col_devices, col_devices, 0)
    own_places = jnp.broadcast_to(positions[None, :], (col_devices, share_rows))
    trace_take, trace_take_ok = jax.vmap(
        lambda r: block_plan(own_trace, own_places, r * col_devices + col_index, capacity)
    )(jnp.arange(row_devices, dtype=jnp.int32))
    trace_take = jnp.where(trace_take_ok, trace_take, -1).transpose(1, 0, 2)
    trace_take = trace_take.reshape(col_devices, 1, row_devices * capacity)
    own_return = lax.dynamic_slice_in_dim(return_blocks, col_index * row_devices, row_devices, 0)
    panel_places = jnp.arange(row_devices, dtype=jnp.int32)[:, None] * share_rows + positions[None, :]
    flux_send = jax.vmap(
        lambda d: block_plan(own_return, panel_places, row_index * col_devices + d, capacity)[0]
    )(jnp.arange(col_devices, dtype=jnp.int32))
    flux_take, flux_take_ok = block_plan(return_blocks, return_slots, device_self, capacity)
    slots = devices * capacity
    trace_send = trace_send.reshape(slots)
    flux_send = flux_send.reshape(col_devices, row_devices * capacity, 1)
    flux_take = jnp.where(flux_take_ok, flux_take, -1).reshape(1, slots)
    face_rows = face_match[:, :, None]

    share = lax.dynamic_slice_in_dim(boundary_start, col_index * share_rows, share_rows, 0)
    share, panel = exchange(False, False, share)
    volume_field = volume_start
    for sweep_index in range(ITERS):
        panel = panel.reshape(row_devices * share_rows, columns)

        volume_flat = volume_field.reshape(elem_count * node_count, columns)
        outgoing = jnp.take(volume_flat, trace_send, axis=0, mode="clip")
        arrived = lax.all_to_all(outgoing, "row", split_axis=0, concat_axis=0, tiled=True)
        arrived = arrived.reshape(row_devices, col_devices, capacity, columns).transpose(1, 0, 2, 3)
        trace_wide = halves(arrived.reshape(col_devices, row_devices * capacity, columns), 2)
        lower_faces = passed_along(volume_field[:, node_count - face_count :, :], ("row", "col"), 1)
        middle = share - boundary_step * (diag_part[:, None] * share - incident)
        operands = (
            halves(panel, 1), trace_wide, trace_take, kernel, elem_mats, volume_field,
            flux_send, flux_take, halves(lower_faces, 2), face_rows, middle,
        )
        if sweep_index < ITERS - 1:
            volume_field, share, panel = exchange(True, False, *operands)
        else:
            volume_field, boundary_final = exchange(True, True, *operands)
    return (boundary_final.reshape(row_panel, columns), volume_field)


def solution(mesh):
    placed = (
        P("row", None),
        P(("row", "col"), None, None),
        P(("row", "col")),
        P(("row", "col"), None),
        P("row", "col"),
        P(("row", "col"), None, None),
        P(),
        P(),
        P(),
        P(),
        P(("row", "col"), None),
    )
    return jax.shard_map(
        shards,
        mesh=mesh,
        in_specs=placed,
        out_specs=(P("row", None), P(("row", "col"), None, None)),
        check_vma=False,
    )
```

profile of v0, /device:TPU:0, one launch (start us, length us, event | category | flops | bytes accessed | tf_op | source)
XLA Modules:
  0.0 320.5 jit_solution(17124526285581899366)
XLA Ops:
  1.8 3.1 collective-permute-start
  6.2 1.6 reduce.12
  7.9 1.6 reduce.13
  10.6 1.2 reduce-window.26
  12.9 5.7 %gather_fusion = f32[1024,128]{1,0:T(8,128)} fusion(f32[4096,128]{1,0:T(8,128)} %bitcast.58, s32[1024]{0:T(1024)S(1)} %broadcast_clamp_fusion), kind=kCustom, calls=%fused_computation | custom fusion | bytes 1052672 | tf_op jit(solution)/shard_map/jit(_take)/gather | solution.py:399
  18.5 4.0 %all-to-all-start = ((f32[4,256,128]{2,1,0:T(8,128)}), f32[4,256,128]{2,1,0:T(8,128)S(1)}, u32[]{:S(2)}, u32[]{:S(2)}) async-start(f32[4,256,128]{2,1,0:T(8,128)} %bitcast.3), calls=%async_computation | async-start | bytes 1048576 | tf_op jit(solution)/shard_map/all_to_all | solution.py:400
  22.8 4.5 %reduce-window.30 = s32[4,8,4,128]{3,1,2,0:T(8,128)S(1)} reduce-window(s32[4,8,4,128]{3,1,2,0:T(8,128)S(1)} %compare_convert_fusion.3, s32[]{:T(128)} %constant.16.clone.1), window={size=1x1x1x128 pad=0_0x0_0x0_0x127_0}, to_apply=%region_3.4 | reduce-window | flops 2080768 | bytes 131076 | tf_op jit(solution)/shard_map/reduce-window.2
  29.4 4.5 %reduce-window.34 = s32[8,4,4,128]{3,0,1,2:T(8,128)S(1)} reduce-window(s32[8,4,4,128]{3,0,1,2:T(8,128)S(1)} %compare_convert_fusion.2, s32[]{:T(128)} %constant.16.clone.1), window={size=1x1x1x128 pad=0_0x0_0x0_0x127_0}, to_apply=%region_7.8 | reduce-window | flops 2080768 | bytes 131076 | tf_op jit(solution)/shard_map/reduce-window.4
  37.2 32.4 %shard_map.122 = (f32[512,128]{1,0:T(8,128)S(1)}, f32[4,512,128]{2,1,0:T(8,128)S(1)}) custom-call(f32[512,128]{1,0:T(8,128)S(1)} %constant_dynamic-slice_fusion.2.refs_0_), custom_call_target="tpu_custom_call" | custom-call | flops 1000 | bytes 150000000 | tf_op jit(solution)/shard_map/pallas_call | solution.py:311
  73.7 68.6 %shard_map.123 = (f32[8,512,128]{2,1,0:T(8,128)}, f32[512,128]{1,0:T(8,128)S(1)}, f32[4,512,128]{2,1,0:T(8,128)S(1)}) custom-call(bf16[2048,256]{1,0:T(8,128)(2,1)S(1)} %pad_maximum_fusion.refs_0_, bf16[8,128,256]{2,1,0:T(8,128)(2,1)S(1)} %pad_maximum_fusion.3.refs_1_, s32[8,1,128]{2,1,0:T(1,128)S(1)} %reshape.216.refs_2_, f32[4096,2048]{1,0:T(8,128)} %refs_3_.5, ...), custom_call_target="tpu_custom_call" | custom-call | flops 1000 | bytes 150000000 | tf_op jit(solution)/shard_map/pallas_call | solution.py:311
  143.2 1.7 slice.42
  144.9 2.0 collective-permute-start.1
  146.9 5.6 %gather_fusion.1 = f32[1024,128]{1,0:T(8,128)} fusion(f32[4096,128]{1,0:T(8,128)} %bitcast.60, s32[1024]{0:T(1024)S(1)} %broadcast_clamp_fusion), kind=kCustom, calls=%fused_computation.1 | custom fusion | bytes 1052672 | tf_op jit(solution)/shard_map/jit(_take)/gather | solution.py:399
  152.5 3.5 %all-to-all-start.1 = ((f32[4,256,128]{2,1,0:T(8,128)}), f32[4,256,128]{2,1,0:T(8,128)S(1)}, u32[]{:S(2)}, u32[]{:S(2)}) async-start(f32[4,256,128]{2,1,0:T(8,128)} %bitcast.16), calls=%async_computation.1 | async-start | bytes 1048576 | tf_op jit(solution)/shard_map/all_to_all | solution.py:400
  158.3 4.2 %all-to-all-done.1 = f32[4,256,128]{2,1,0:T(8,128)S(1)} async-done(((f32[4,256,128]{2,1,0:T(8,128)}), f32[4,256,128]{2,1,0:T(8,128)S(1)}, u32[]{:S(2)}, u32[]{:S(2)}) %all-to-all-start.1) | async-done | bytes 524320 | tf_op jit(solution)/shard_map/all_to_all | solution.py:400
  162.7 70.4 %shard_map.124 = (f32[8,512,128]{2,1,0:T(8,128)}, f32[512,128]{1,0:T(8,128)S(1)}, f32[4,512,128]{2,1,0:T(8,128)S(1)}) custom-call(bf16[2048,256]{1,0:T(8,128)(2,1)S(1)} %pad_maximum_fusion.1.refs_0_, bf16[8,128,256]{2,1,0:T(8,128)(2,1)S(1)} %pad_maximum_fusion.4.refs_1_, s32[8,1,128]{2,1,0:T(1,128)S(1)} %reshape.216.refs_2_, f32[4096,2048]{1,0:T(8,128)} %refs_3_.5, ...), custom_call_target="tpu_custom_call" | custom-call | flops 1000 | bytes 150000000 | tf_op jit(solution)/shard_map/pallas_call | solution.py:311
  234.1 1.7 slice.43
  235.8 2.0 collective-permute-start.2
  237.8 5.6 %gather_fusion.2 = f32[1024,128]{1,0:T(8,128)} fusion(f32[4096,128]{1,0:T(8,128)} %bitcast.59, s32[1024]{0:T(1024)S(1)} %broadcast_clamp_fusion), kind=kCustom, calls=%fused_computation.2 | custom fusion | bytes 1052672 | tf_op jit(solution)/shard_map/jit(_take)/gather | solution.py:399
  243.4 3.7 %all-to-all-start.2 = ((f32[4,256,128]{2,1,0:T(8,128)}), f32[4,256,128]{2,1,0:T(8,128)S(1)}, u32[]{:S(2)}, u32[]{:S(2)}) async-start(f32[4,256,128]{2,1,0:T(8,128)} %bitcast.22), calls=%async_computation.2 | async-start | bytes 1048576 | tf_op jit(solution)/shard_map/all_to_all | solution.py:400
  249.5 4.0 %all-to-all-done.2 = f32[4,256,128]{2,1,0:T(8,128)S(1)} async-done(((f32[4,256,128]{2,1,0:T(8,128)}), f32[4,256,128]{2,1,0:T(8,128)S(1)}, u32[]{:S(2)}, u32[]{:S(2)}) %all-to-all-start.2) | async-done | bytes 524320 | tf_op jit(solution)/shard_map/all_to_all | solution.py:400
  253.7 62.2 %shard_map.125 = (f32[8,512,128]{2,1,0:T(8,128)S(1)}, f32[8,512,128]{2,1,0:T(8,128)}) custom-call(bf16[2048,256]{1,0:T(8,128)(2,1)S(1)} %pad_maximum_fusion.2.refs_0_, bf16[8,128,256]{2,1,0:T(8,128)(2,1)S(1)} %pad_maximum_fusion.5.refs_1_, s32[8,1,128]{2,1,0:T(1,128)S(1)} %reshape.216.refs_2_, f32[4096,2048]{1,0:T(8,128)} %refs_3_.5, ...), custom_call_target="tpu_custom_call" | custom-call | flops 1000 | bytes 150000000 | tf_op jit(solution)/shard_map/pallas_call | solution.py:311
  315.9 3.2 copy.60
  319.1 1.3 copy.61
  (99 shorter events, 21.0 us)
Async XLA Ops:
  0.6 36.5 %copy-start = (f32[4096,128]{1,0:T(8,128)S(1)}, f32[4096,128]{1,0:T(8,128)}, u32[]{:S(2)}) copy-start(f32[4096,128]{1,0:T(8,128)} %param.11) | copy-start | bytes 6291460
  1.8 70.6 %collective-permute-start = (f32[8,64,128]{2,1,0:T(8,128)S(1)}, f32[8,64,128]{2,1,0:T(8,128)}, u32[]{:S(2)}, u32[]{:S(2)}) collective-permute-start(f32[8,64,128]{2,1,0:T(8,128)S(1)} %slice.41), channel_id=1, source_target_pairs={{0,1},{1,2},{2,3},{3,4},{4,5},{5,6},{6,7},{7,8},{8,9},{9,10},{10,1... | collective-permute-start | bytes 786440 | tf_op jit(solution)/shard_map/ppermute | solution.py:21
  12.9 16.3 %copy-start.3 = (s32[16384]{0:T(1024)S(1)}, s32[16384]{0:T(1024)}, u32[]{:S(2)}) copy-start(s32[16384]{0:T(1024)} %param.20) | copy-start | bytes 196612
  18.5 54.9 %all-to-all-start = ((f32[4,256,128]{2,1,0:T(8,128)}), f32[4,256,128]{2,1,0:T(8,128)S(1)}, u32[]{:S(2)}, u32[]{:S(2)}) async-start(f32[4,256,128]{2,1,0:T(8,128)} %bitcast.3), calls=%async_computation | async-start | bytes 1048576 | tf_op jit(solution)/shard_map/all_to_all | solution.py:400
  69.6 1.0 copy-start.2
  69.6 0.9 copy-start.4
  69.8 1.9 copy-start.5
  144.9 12.4 %collective-permute-start.1 = (f32[8,64,128]{2,1,0:T(8,128)}, f32[8,64,128]{2,1,0:T(8,128)}, u32[]{:S(2)}, u32[]{:S(2)}) collective-permute-start(f32[8,64,128]{2,1,0:T(8,128)} %slice.42), channel_id=1, source_target_pairs={{0,1},{1,2},{2,3},{3,4},{4,5},{5,6},{6,7},{7,8},{8,9},{9,10},{10,1... | collective-permute-start | bytes 786440 | tf_op jit(solution)/shard_map/ppermute | solution.py:21
  152.5 10.0 %all-to-all-start.1 = ((f32[4,256,128]{2,1,0:T(8,128)}), f32[4,256,128]{2,1,0:T(8,128)S(1)}, u32[]{:S(2)}, u32[]{:S(2)}) async-start(f32[4,256,128]{2,1,0:T(8,128)} %bitcast.16), calls=%async_computation.1 | async-start | bytes 1048576 | tf_op jit(solution)/shard_map/all_to_all | solution.py:400
  235.8 12.7 %collective-permute-start.2 = (f32[8,64,128]{2,1,0:T(8,128)}, f32[8,64,128]{2,1,0:T(8,128)}, u32[]{:S(2)}, u32[]{:S(2)}) collective-permute-start(f32[8,64,128]{2,1,0:T(8,128)} %slice.43), channel_id=1, source_target_pairs={{0,1},{1,2},{2,3},{3,4},{4,5},{5,6},{6,7},{7,8},{8,9},{9,10},{10,1... | collective-permute-start | bytes 786440 | tf_op jit(solution)/shard_map/ppermute | solution.py:21
  243.4 10.1 %all-to-all-start.2 = ((f32[4,256,128]{2,1,0:T(8,128)}), f32[4,256,128]{2,1,0:T(8,128)S(1)}, u32[]{:S(2)}, u32[]{:S(2)}) async-start(f32[4,256,128]{2,1,0:T(8,128)} %bitcast.22), calls=%async_computation.2 | async-start | bytes 1048576 | tf_op jit(solution)/shard_map/all_to_all | solution.py:400
  315.9 4.5 %copy-start.1 = (f32[4096,128]{1,0:T(8,128)S(1)}, f32[4096,128]{1,0:T(8,128)}, u32[]{:S(2)}) copy-start(f32[4096,128]{1,0:T(8,128)} %param.11) | copy-start | bytes 6291460
where the time goes:
time: 326 us; the launch traced here: 320 us
  Pallas kernels  234 us (72%)
  local copies, waits for them, and re-layouts  30.3 us (9%)
  other arithmetic  28.9 us (9%)
  starting transfers between devices  18.3 us (6%)
  waiting for transfers between devices  8.15 us (2%)
    pallas_call x4, Pallas kernels, exchange(): pl.pallas_call(functools.partial(exchange_kernel, reduces, finishes), out...  234 us
    gather x3, local copies, waits for them, and re-layouts, shards(): outgoing = jnp.take(volume_flat, trace_send, axis=0, mode='clip')  16.9 us
    another operation x8, other arithmetic  11.5 us
    all_to_all x3, starting transfers between devices, shards(): lax.all_to_all(outgoing, 'row', split_axis=0, concat_axis=0, tiled=True)  11.2 us
    all_to_all x3, waiting for transfers between devices, shards(): lax.all_to_all(outgoing, 'row', split_axis=0, concat_axis=0, tiled=True)  8.14 us
    ppermute x3, starting transfers between devices, passed_along(): return lax.ppermute(block, axis, route)  7.07 us
  transfers between devices with their start and end apart: 6, of which 2 were waited for; matrix products, arithmetic and copies ran while one was open for 15% of the time, Pallas kernels for 10%

commit v1 on v0

v1 whole, which is shorter than its diff:
```python
import functools

import jax
import jax.numpy as jnp
from jax import lax
from jax.experimental import pallas as pl
from jax.experimental.pallas import tpu as pltpu
from jax.sharding import PartitionSpec as P

ITERS = 3


boundary_step = 0.5
volume_step = 0.6
face_weight = 0.5


def parts(block):
    high = block.astype(jnp.bfloat16)
    low = (block - high.astype(jnp.float32)).astype(jnp.bfloat16)
    return high, low


def wide_of(block):
    return jnp.concatenate(parts(block), axis=1)


def product(left, right):
    return jnp.dot(left, right, preferred_element_type=jnp.float32)


def one_hot(hits):
    return jnp.where(hits, 1.0, 0.0).astype(jnp.bfloat16)


def sweeps_kernel(*refs):
    boundary_start, volume_start, kernel, elem_mats, diag, incident = refs[:6]
    trace_send, trace_take, flux_send, flux_take, face_rows = refs[6:11]
    volume, out = refs[11:13]
    (
        kernel_held, elem_held, share, panels, panel_wide, partial, from_pair, from_line,
        flux_leaving, flux_landed, flux_wide, trace_leaving, trace_landed, trace_wide, faces,
    ) = refs[13:28]
    (
        kernel_sem, elem_sem, volume_sem, share_sem, move_send, move_recv, row_send, row_recv,
        pair_send, pair_recv, line_send, line_recv, flux_out, flux_in, trace_out, trace_in,
        face_out, face_in, out_sem, final_send, final_recv, back_send, back_recv,
    ) = refs[28:]

    rows_n, cols_n = lax.axis_size("row"), lax.axis_size("col")
    pairs = cols_n // 2
    per_panel = cols_n // rows_n
    r, c = lax.axis_index("row"), lax.axis_index("col")
    z, h = c // 2, c % 2
    partner = z * 2 + (1 - h)
    target_row, target_col = c % rows_n, r * per_panel + c // rows_n
    source_row, source_col = c // per_panel, (c % per_panel) * rows_n + r
    stays = (target_row == r) & (target_col == c)
    moves = jnp.logical_not(stays)
    device = r * cols_n + c
    has_next, has_prev = device < rows_n * cols_n - 1, device > 0
    next_row, next_col = (device + 1) // cols_n, (device + 1) % cols_n

    share_rows, columns = share.shape
    elem_count, node_count = elem_held.shape[:2]
    face_count = faces.shape[2]
    capacity = flux_leaving.shape[2]
    slots = flux_wide.shape[0]
    above = pairs - 1 - z

    def target(k):
        return jnp.where(k < above, pairs - 1 - k, k - above)

    def block_of(i):
        t = target(i // 2)
        return t * 2 + jnp.where(i % 2 == 0, 1 - h, h)

    def load(i):
        b = block_of(i)
        return pltpu.make_async_copy(
            kernel.at[pl.ds(pl.multiple_of(b * share_rows, share_rows), share_rows), :],
            kernel_held.at[b], kernel_sem.at[i],
        )

    share_load = pltpu.make_async_copy(
        boundary_start.at[pl.ds(pl.multiple_of(c * share_rows, share_rows), share_rows), :], share, share_sem
    )
    volume_load = pltpu.make_async_copy(volume_start, volume, volume_sem)
    elem_load = pltpu.make_async_copy(elem_mats, elem_held, elem_sem)
    share_load.start()
    volume_load.start()
    for i in range(cols_n):
        load(i).start()
    elem_load.start()

    barrier = pltpu.get_barrier_semaphore()

    def greet(row, col):
        pl.semaphore_signal(barrier, inc=1, device_id=(row, col), device_id_type=pl.DeviceIdType.MESH)

    for step in range(1, cols_n):
        greet(r, (c + step) % cols_n)
    for step in range(1, rows_n):
        greet((r + step) % rows_n, c)

    @pl.when(moves)
    def _():
        greet(source_row, source_col)

    @pl.when((c == 0) & (r > 0))
    def _():
        greet(r - 1, cols_n - 1)

    greeted = cols_n - 1 + rows_n - 1 + jnp.where(stays, 0, 1)
    greeted += jnp.where((c == cols_n - 1) & (r < rows_n - 1), 1, 0)
    pl.semaphore_wait(barrier, greeted)

    def remote(src, dst, send, recv, row, col):
        return pltpu.make_async_remote_copy(
            src_ref=src, dst_ref=dst, send_sem=send, recv_sem=recv,
            device_id=(row, col), device_id_type=pl.DeviceIdType.MESH,
        )

    def move(par):
        return remote(
            share, panels.at[par, target_row], move_send, move_recv.at[par], target_row, target_col
        )

    def row_copy(par, step):
        piece = panels.at[par, r]
        return remote(
            piece, piece, row_send.at[step - 1], row_recv.at[par, step - 1], (r + step) % rows_n, c
        )

    def pair_copy(par, t):
        return remote(
            partial.at[t * 2 + (1 - h)], from_pair.at[par, t], pair_send.at[t], pair_recv.at[par, t], r, partner
        )

    def up_copy(par, t):
        return remote(
            partial.at[t * 2 + h], from_line.at[par, t + 1],
            line_send.at[t + 1], line_recv.at[par, t + 1], r, c + 2,
        )

    def down_copy(par, t):
        return remote(
            partial.at[t * 2 + h], from_line.at[par, t], line_send.at[t], line_recv.at[par, t], r, c - 2
        )

    def flux_copy(par, piece, step):
        member = (c + step) % cols_n
        return remote(
            flux_leaving.at[piece, member], flux_landed.at[par, c, piece],
            flux_out.at[piece, step - 1], flux_in.at[par, piece, step - 1], r, member,
        )

    def trace_copy(par, step):
        row = (r + step) % rows_n
        return remote(
            trace_leaving.at[row], trace_landed.at[par, r], trace_out.at[step - 1],
            trace_in.at[par, step - 1], row, c,
        )

    def face_copy(par, e):
        start = pl.multiple_of(e * node_count + (node_count - face_count), 8)
        return remote(
            volume.at[pl.ds(start, face_count), :], faces.at[par, e],
            face_out.at[e], face_in.at[par, e], next_row, next_col,
        )

    def send_faces(par):
        @pl.when(has_next)
        def _():
            for e in range(elem_count):
                face_copy(par, e).start()

    def wait_faces_sent(par):
        @pl.when(has_next)
        def _():
            for e in range(elem_count):
                face_copy(par, e).wait_send()

    def send_traces(par):
        def pick(row, k, carry):
            for p in range(capacity):
                slot = trace_send[(row * cols_n + k) * capacity + p]
                trace_leaving[row, k, pl.ds(p, 1), :] = volume[pl.ds(slot, 1), :]
            return carry

        for step in range(1, rows_n):
            lax.fori_loop(0, cols_n, functools.partial(pick, (r + step) % rows_n), 0)
            trace_copy(par, step).start()
        lax.fori_loop(0, cols_n, functools.partial(pick, r), 0)
        trace_landed[par, r] = trace_leaving[r]

    def wait_traces_sent(par):
        for step in range(1, rows_n):
            trace_copy(par, step).wait_send()

    def relay_up(par, t):
        up_copy(par, t).start()

    def relay_down(par, t):
        down_copy(par, t).start()

    def take_piece(par, step, carry):
        piece = (r + rows_n - step) % rows_n

        @pl.when(step > 0)
        def _():
            row_copy(par, jnp.maximum(step, 1)).wait_recv()

        wide = wide_of(panels[par, piece])
        panel_wide[pl.ds(pl.multiple_of(piece * share_rows, share_rows), share_rows), :] = wide
        place = lax.broadcasted_iota(jnp.int32, (cols_n * capacity, share_rows), 1)
        picked = product(one_hot(place == flux_send[piece]), wide)
        picked = picked[:, :columns] + picked[:, columns:]
        flux_leaving[piece] = picked.reshape(cols_n, capacity, columns)
        for other in range(1, cols_n):
            flux_copy(par, piece, other).start()
        flux_landed[par, c, piece] = flux_leaving[piece, c]
        return carry

    def product_step(s, par, i, carry):
        b = block_of(i)
        t = target(i // 2)

        @pl.when(s == 0)
        def _():
            load(i).wait()

        high, low = parts(kernel_held[b])
        place = lax.broadcasted_iota(jnp.int32, (share_rows, trace_wide.shape[1]), 0)
        wide = product(high, panel_wide[...]) + product(low, panel_wide[...])
        wide -= product(one_hot(place == trace_take[b]), trace_wide[b])
        partial[b] = wide[:, :columns] + wide[:, columns:]

        @pl.when(i % 2 == 0)
        def _():
            pair_copy(par, t).start()

        @pl.when(i % 2 == 1)
        def _():
            pair_copy(par, t).wait_recv()
            partial[b] += from_pair[par, t]

            @pl.when((z == 0) & (t > z))
            def _():
                up_copy(par, t).start()

            @pl.when((z == pairs - 1) & (t < z))
            def _():
                down_copy(par, t).start()

        return carry

    def volume_step_of(par, e, carry):
        nodes = pl.ds(pl.multiple_of(e * node_count, node_count), node_count)
        field = volume[nodes, :]
        high, low = parts(elem_held[e])
        field_wide = wide_of(field)
        wide = product(high, field_wide) + product(low, field_wide)
        place = lax.broadcasted_iota(jnp.int32, (node_count, slots), 0) + e * node_count
        wide -= product(one_hot(place == flux_take[...]), flux_wide[...])
        volume[nodes, :] = field - volume_step * (field + wide[:, :columns] + wide[:, columns:])
        node = lax.broadcasted_iota(jnp.int32, (face_count, face_count), 1)
        face = product(one_hot(node == face_rows[e]), wide_of(faces[par, e]))
        matched = face[:, :columns] + face[:, columns:]
        lower = pl.ds(pl.multiple_of(e * node_count, node_count), face_count)
        volume[lower, :] += volume_step * face_weight * matched
        return carry

    gaps = max(1, pairs - 2)
    chunk = -(-elem_count // gaps)

    def relay_step(par, stage, carry):
        @pl.when((z >= 1) & (z <= stage) & (stage <= pairs - 2))
        def _():
            t = pairs - 1 + z - stage
            up_copy(par, t - 0).wait_recv()
            partial[t * 2 + h] += from_line[par, t + 1]
            up_copy(par, t).start()

        @pl.when((z <= pairs - 2) & (above <= stage) & (stage <= pairs - 2))
        def _():
            t = stage - above
            down_copy(par, t).wait_recv()
            partial[t * 2 + h] += from_line[par, t]
            down_copy(par, t).start()

        first = jnp.minimum((stage - 1) * chunk, elem_count)
        last = jnp.minimum(stage * chunk, elem_count)
        lax.fori_loop(first, last, functools.partial(volume_step_of, par), 0)
        return carry

    def sweep(s, carry):
        par = s % 2
        lax.fori_loop(0, rows_n, functools.partial(take_piece, par), 0)

        for step in range(1, rows_n):
            trace_copy(par, step).wait_recv()
        for b in range(cols_n):
            landed = trace_landed[par, :, b].reshape(rows_n * capacity, columns)
            trace_wide[b] = wide_of(landed)

        lax.fori_loop(0, cols_n, functools.partial(product_step, s, par), 0)

        @pl.when(s == 0)
        def _():
            elem_load.wait()

        for piece in range(rows_n):
            for other in range(1, cols_n):
                flux_copy(par, piece, other).wait_recv()
        flux_wide[...] = wide_of(flux_landed[par].reshape(slots, columns))

        @pl.when(has_prev)
        def _():
            for e in range(elem_count):
                face_copy(par, e).wait_recv()

        wait_faces_sent(par)
        wait_traces_sent(par)
        lax.fori_loop(1, 1 + gaps, functools.partial(relay_step, par), 0)

        @pl.when(s < ITERS - 1)
        def _():
            send_faces(1 - par)
            send_traces(1 - par)

        own = z * 2 + h

        @pl.when(z > 0)
        def _():
            up_copy(par, z).wait_recv()
            partial[own] += from_line[par, z + 1]

        @pl.when(z < pairs - 1)
        def _():
            down_copy(par, z).wait_recv()
            partial[own] += from_line[par, z]

        @pl.when(moves)
        def _():
            move(par).wait_send()

        held = share[...]
        middle = held - boundary_step * (diag[...] * held - incident[...])
        share[...] = middle - boundary_step * partial[own]

        @pl.when((s < ITERS - 1) & moves)
        def _():
            move(1 - par).start()

        for step in range(1, rows_n):
            row_copy(par, step).wait_send()
        for t in range(pairs):
            pair_copy(par, t).wait_send()

            @pl.when(t > z)
            def _():
                up_copy(par, t).wait_send()

            @pl.when(t < z)
            def _():
                down_copy(par, t).wait_send()

        for piece in range(rows_n):
            for other in range(1, cols_n):
                flux_copy(par, piece, other).wait_send()

        @pl.when(s < ITERS - 1)
        def _():
            finish_spread(1 - par)

        return carry

    def finish_spread(par):
        @pl.when(stays)
        def _():
            panels[par, r] = share[...]

        @pl.when(moves)
        def _():
            move(par).wait_recv()

        for step in range(1, rows_n):
            row_copy(par, step).start()

    share_load.wait()

    @pl.when(moves)
    def _():
        move(0).start()

    @pl.when(jnp.logical_not(has_prev))
    def _():
        faces[...] = jnp.zeros_like(faces)

    volume_load.wait()
    send_faces(0)
    send_traces(0)
    finish_spread(0)
    lax.fori_loop(0, ITERS, sweep, 0)

    keep = pltpu.make_async_copy(share, out.at[c], out_sem)
    keep.start()

    def final_up(src, origin, step):
        return remote(
            src, out.at[origin], final_send.at[0, step - 1], final_recv.at[0, step - 1], r, c + 2
        )

    def final_down(src, origin, step):
        return remote(
            src, out.at[origin], final_send.at[1, step - 1], final_recv.at[1, step - 1], r, c - 2
        )

    def back(src, origin, place):
        return remote(src, out.at[origin], back_send.at[place], back_recv.at[place], r, partner)

    @pl.when(z < pairs - 1)
    def _():
        final_up(share, c, 1).start()

    @pl.when(z > 0)
    def _():
        final_down(share, c, 1).start()

    back(share, c, z).start()
    for step in range(1, pairs):
        lower, upper = c - 2 * step, c + 2 * step

        @pl.when(z >= step)
        def _():
            final_up(share, lower, step).wait_recv()

            @pl.when(z < pairs - 1)
            def _():
                final_up(out.at[lower], lower, step + 1).start()

            back(out.at[lower], lower, z - step).start()

        @pl.when(z + step < pairs)
        def _():
            final_down(share, upper, step).wait_recv()

            @pl.when(z > 0)
            def _():
                final_down(out.at[upper], upper, step + 1).start()

            back(out.at[upper], upper, z + step).start()

    keep.wait()
    for place in range(pairs):
        back(share, c, place).wait_recv()
    for place in range(pairs):
        back(share, c, place).wait_send()
    for step in range(1, pairs + 1):
        @pl.when((z < pairs - 1) & (z >= step - 1))
        def _():
            final_up(share, c, step).wait_send()

        @pl.when((z > 0) & (z + step - 1 < pairs))
        def _():
            final_down(share, c, step).wait_send()


def sweeps(boundary_start, volume_flat, kernel, elem_mats, diag, incident, plans, capacity, face_rows):
    rows_n, cols_n = lax.axis_size("row"), lax.axis_size("col")
    pairs = cols_n // 2
    share_rows, columns = incident.shape
    panel_rows = kernel.shape[1]
    elem_count, face_count = face_rows.shape[:2]
    block = (share_rows, columns)
    slots = rows_n * cols_n * capacity
    f32, bf16 = jnp.float32, jnp.bfloat16
    in_vmem, anywhere = pl.BlockSpec(memory_space=pltpu.VMEM), pl.BlockSpec(memory_space=pl.ANY)
    in_smem = pl.BlockSpec(memory_space=pltpu.SMEM)
    dma = pltpu.SemaphoreType.DMA
    scratch = [
        pltpu.VMEM((cols_n, share_rows, panel_rows), f32),
        pltpu.VMEM(elem_mats.shape, f32),
        pltpu.VMEM(block, f32),
        pltpu.VMEM((2, rows_n) + block, f32),
        pltpu.VMEM((panel_rows, 2 * columns), bf16),
        pltpu.VMEM((cols_n,) + block, f32),
        pltpu.VMEM((2, pairs) + block, f32),
        pltpu.VMEM((2, pairs + 1) + block, f32),
        pltpu.VMEM((rows_n, cols_n, capacity, columns), f32),
        pltpu.VMEM((2, cols_n, rows_n, capacity, columns), f32),
        pltpu.VMEM((slots, 2 * columns), bf16),
        pltpu.VMEM((rows_n, cols_n, capacity, columns), f32),
        pltpu.VMEM((2, rows_n, cols_n, capacity, columns), f32),
        pltpu.VMEM((cols_n, rows_n * capacity, 2 * columns), bf16),
        pltpu.VMEM((2, elem_count, face_count, columns), f32),
        dma((cols_n,)), dma, dma, dma,
        dma, dma((2,)), dma((rows_n - 1,)), dma((2, rows_n - 1)),
        dma((pairs,)), dma((2, pairs)), dma((pairs + 1,)), dma((2, pairs + 1)),
        dma((rows_n, cols_n - 1)), dma((2, rows_n, cols_n - 1)),
        dma((rows_n - 1,)), dma((2, rows_n - 1)),
        dma((elem_count,)), dma((2, elem_count)),
        dma, dma((2, pairs)), dma((2, pairs)), dma((pairs,)), dma((pairs,)),
    ]
    return pl.pallas_call(
        sweeps_kernel,
        out_shape=[
            jax.ShapeDtypeStruct(volume_flat.shape, f32),
            jax.ShapeDtypeStruct((cols_n,) + block, f32),
        ],
        in_specs=[anywhere] * 4 + [in_vmem] * 2 + [in_smem] + [in_vmem] * 4,
        out_specs=[in_vmem, anywhere],
        scratch_shapes=scratch,
        compiler_params=pltpu.CompilerParams(
            collective_id=0, has_side_effects=True, vmem_limit_bytes=67043328
        ),
        cost_estimate=pl.CostEstimate(flops=1000, bytes_accessed=150_000_000, transcendentals=0),
    )(boundary_start, volume_flat, kernel, elem_mats, diag, incident, *plans, face_rows)


def shards(
    boundary_start,
    volume_start,
    diag_part,
    incident,
    kernel,
    elem_mats,
    trace_owner,
    trace_slot,
    return_owner,
    return_slot,
    face_match,
):
    rows_n, cols_n = lax.axis_size("row"), lax.axis_size("col")
    devices = rows_n * cols_n
    r, c = lax.axis_index("row"), lax.axis_index("col")
    device = r * cols_n + c
    share_rows = trace_slot.shape[0] // devices
    capacity = max(2, 2 * share_rows // devices)
    elem_count, node_count, columns = volume_start.shape

    trace_blocks = trace_owner[:, 0].reshape(devices, share_rows)
    trace_slots = trace_slot.reshape(devices, share_rows)
    return_blocks = return_owner[:, 0].reshape(devices, share_rows)
    return_slots = return_slot.reshape(devices, share_rows)
    own_trace = lax.dynamic_slice_in_dim(trace_blocks, r * cols_n, cols_n, 0)
    own_return = lax.dynamic_slice_in_dim(return_blocks, c * rows_n, rows_n, 0)
    row_owners = jnp.arange(rows_n, dtype=jnp.int32) * cols_n + c
    col_owners = r * cols_n + jnp.arange(cols_n, dtype=jnp.int32)
    masks = jnp.concatenate([
        trace_blocks == device,
        (own_trace[:, None, :] == row_owners[None, :, None]).reshape(devices, share_rows),
        (own_return[:, None, :] == col_owners[None, :, None]).reshape(devices, share_rows),
        return_blocks == device,
    ])
    places = jnp.broadcast_to(jnp.arange(share_rows, dtype=jnp.int32)[None, :], (2 * devices, share_rows))
    values = jnp.concatenate([trace_slots, places, return_slots]) + 1
    earlier = jnp.triu(jnp.ones((share_rows, share_rows), jnp.bfloat16))
    ranks = jnp.dot(masks.astype(jnp.bfloat16), earlier, preferred_element_type=jnp.float32)
    ranks = jnp.where(masks, ranks, 0.0)
    wanted = jnp.arange(1, capacity + 1, dtype=jnp.int32).astype(jnp.float32)
    hits = ranks[:, None, :] == wanted[None, :, None]
    plan = jnp.sum(jnp.where(hits, values[:, None, :], 0), axis=2) - 1
    plan = plan.reshape(4, devices * capacity)
    plans = (
        jnp.maximum(plan[0], 0),
        plan[1].reshape(cols_n, 1, rows_n * capacity),
        plan[2].reshape(rows_n, cols_n * capacity, 1),
        plan[3].reshape(1, devices * capacity),
    )
    volume_final, boundary_final = sweeps(
        boundary_start, volume_start.reshape(elem_count * node_count, columns), kernel, elem_mats,
        diag_part[:, None], incident, plans, capacity, face_match[:, :, None],
    )
    return (
        boundary_final.reshape(boundary_start.shape),
        volume_final.reshape(volume_start.shape),
    )


def solution(mesh):
    placed = (
        P("row", None),
        P(("row", "col"), None, None),
        P(("row", "col")),
        P(("row", "col"), None),
        P("row", "col"),
        P(("row", "col"), None, None),
        P(),
        P(),
        P(),
        P(),
        P(("row", "col"), None),
    )
    return jax.shard_map(
        shards,
        mesh=mesh,
        in_specs=placed,
        out_specs=(P("row", None), P(("row", "col"), None, None)),
        check_vma=False,
    )
```

time: 326 us -> 226 us (0.69); the launches traced: 320 us -> 226 us
  Pallas kernels: 234 us -> 204 us
  other arithmetic: 28.9 us -> 5.78 us
  starting transfers between devices: 18.3 us -> 0 us
  local copies, waits for them, and re-layouts: 30.3 us -> 15 us
  waiting for transfers between devices: 8.15 us -> 0 us
    pallas_call x4 -> x1, Pallas kernels: 234 us -> 204 us  [sweeps(): pl.pallas_call(sweeps_kernel, out_shape=[jax.ShapeDtypeStruct(volume_flat...]
    gather x3 -> x0, local copies, waits for them, and re-layouts: 16.9 us -> none  [shards(): outgoing = jnp.take(volume_flat, trace_send, axis=0, mode='clip')]
    another operation x8 -> x0, other arithmetic: 11.5 us -> none
    all_to_all x3 -> x0, starting transfers between devices: 11.2 us -> none  [shards(): lax.all_to_all(outgoing, 'row', split_axis=0, concat_axis=0, tiled=True)]
    all_to_all x3 -> x0, waiting for transfers between devices: 8.14 us -> none  [shards(): lax.all_to_all(outgoing, 'row', split_axis=0, concat_axis=0, tiled=True)]
    ppermute x3 -> x0, starting transfers between devices: 7.07 us -> none  [passed_along(): return lax.ppermute(block, axis, route)]
    convert_element_type x12 -> x1, other arithmetic: 6.5 us -> 0.01 us  [shards(): wanted = jnp.arange(1, capacity + 1, dtype=jnp.int32).astype(jnp.float32)]
    slice x4 -> x1, local copies, waits for them, and re-layouts: 4.7 us -> 0.67 us  [shards(): plan[3].reshape(1, devices * capacity)]
  transfers between devices with their start and end apart: 6 -> 0, of which waited for: 2 -> 0; matrix products, arithmetic and copies ran while one was open for 15% -> 0% of each run, Pallas kernels for 10% -> 0%
where the time goes in v1:
time: 226 us
  Pallas kernels  204 us (90%)
  local copies, waits for them, and re-layouts  15 us (7%)
  other arithmetic  5.78 us (3%)
    pallas_call x1, Pallas kernels, sweeps(): pl.pallas_call(sweeps_kernel, out_shape=[jax.ShapeDtypeStruct(volume_flat...  204 us
    unnamed x3, local copies, waits for them, and re-layouts  6.62 us

profile of v1, /device:TPU:0, one launch (start us, length us, event | category | flops | bytes accessed | tf_op | source)
XLA Modules:
  0.0 225.8 jit_solution(17914007659783260973)
XLA Ops:
  0.7 0.1 eq.74
  0.8 0.1 eq.68
  0.9 0.5 broadcast.50
  1.4 1.6 reduce.7
  3.1 1.6 reduce.6
  4.8 0.1 bitcast_compare_fusion
  4.9 0.9 concatenate.15
  5.8 0.9 concatenate.16
  6.7 0.3 convolution_select_fusion
  7.0 2.3 %select_reduce_fusion = s32[128,32]{1,0:T(8,128)S(1)} fusion(s32[128,512]{1,0:T(8,128)S(1)} %add_add_fusion, f32[128,512]{1,0:T(8,128)S(1)} %convolution_select_fusion, f32[32]{0:T(128)S(1)} %add_convert_fusion), kind=kLoop, calls=%fused_computation | loop fusion | flops 6287360 | bytes 540800 | tf_op jit(solution)/shard_map/reduce_sum | solution.py:564
  9.4 0.7 slice.22.refs_9_
  10.0 0.7 reshape_squeeze.14.refs_7_
  10.7 0.7 max.10.refs_6_
  11.4 1.5 copy.16.refs_4_
  12.9 1.5 copy.18.refs_10_
  14.4 1.3 reshape_squeeze.16.refs_8_
  15.8 204.0 %shard_map.122 = (f32[4096,128]{1,0:T(8,128)}, f32[8,512,128]{2,1,0:T(8,128)}) custom-call(f32[4096,128]{1,0:T(8,128)} %refs_0_.1, f32[4096,128]{1,0:T(8,128)} %bitcast.9, f32[4096,2048]{1,0:T(8,128)} %refs_2_.1, f32[8,512,512]{2,1,0:T(8,128)} %refs_3_.1, f32[512,1]{1,0:T(8,128)} %copy.16.refs_4_, f32[512,128]{1,0:T(8,128)} %refs_5_.1, s32[1024]{0:T(1024)} %max.10.refs_6_, ...), custom_call_target="tpu_custom_call" | custom-call | flops 1000 | bytes 150000000 | tf_op jit(solution)/shard_map/pallas_call | solution.py:506
  219.7 3.0 %copy.33 = f32[4096,128]{1,0:T(8,128)} copy(f32[4096,128]{1,0:T(8,128)} %bitcast.11) | data formatting | bytes 4194304
  222.8 3.1 %copy.34 = f32[8,512,128]{2,1,0:T(8,128)} copy(f32[8,512,128]{2,1,0:T(8,128)} %bitcast.10) | data formatting | bytes 4194304
  (17 shorter events, 0.2 us)

commit v2 on v1

--- a/solution.py
+++ b/solution.py
@@ -34,63 +34,80 @@
 
 
 def sweeps_kernel(*refs):
-    boundary_start, volume_start, kernel, elem_mats, diag, incident = refs[:6]
+    boundary_start, volume_start, kernel, elem_mats, diag_own, incident_own = refs[:6]
     trace_send, trace_take, flux_send, flux_take, face_rows = refs[6:11]
     volume, out = refs[11:13]
     (
-        kernel_held, elem_held, share, panels, panel_wide, partial, from_pair, from_line,
-        flux_leaving, flux_landed, flux_wide, trace_leaving, trace_landed, trace_wide, faces,
-    ) = refs[13:28]
+        kernel_held, elem_held, diag_row, diag, incident, middle_out, middle, panels, panel_wide, partial, from_pair,
+        from_row, from_line, flux_leaving, flux_landed, flux_wide, trace_leaving, trace_landed, trace_wide, faces,
+    ) = refs[13:33]
     (
-        kernel_sem, elem_sem, volume_sem, share_sem, move_send, move_recv, row_send, row_recv,
-        pair_send, pair_recv, line_send, line_recv, flux_out, flux_in, trace_out, trace_in,
+        kernel_sem, elem_sem, volume_sem, piece_sem, move_send, move_recv, start_send, start_recv, row_send, row_recv,
+        pair_send, pair_recv, turn_send, turn_recv, line_send, line_recv, flux_out, flux_in, trace_out, trace_in,
         face_out, face_in, out_sem, final_send, final_recv, back_send, back_recv,
-    ) = refs[28:]
+    ) = refs[33:]
 
     rows_n, cols_n = lax.axis_size("row"), lax.axis_size("col")
     pairs = cols_n // 2
-    per_panel = cols_n // rows_n
+    assert rows_n == pairs
     r, c = lax.axis_index("row"), lax.axis_index("col")
     z, h = c // 2, c % 2
     partner = z * 2 + (1 - h)
-    target_row, target_col = c % rows_n, r * per_panel + c // rows_n
-    source_row, source_col = c // per_panel, (c % per_panel) * rows_n + r
+    target_row, target_col = c % rows_n, r * 2 + c // rows_n
+    source_row, source_col = z, h * rows_n + r
     stays = (target_row == r) & (target_col == c)
     moves = jnp.logical_not(stays)
     device = r * cols_n + c
     has_next, has_prev = device < rows_n * cols_n - 1, device > 0
     next_row, next_col = (device + 1) // cols_n, (device + 1) % cols_n
-
-    share_rows, columns = share.shape
+    roots = r == z
+
+    share_rows, columns = middle.shape
     elem_count, node_count = elem_held.shape[:2]
     face_count = faces.shape[2]
     capacity = flux_leaving.shape[2]
     slots = flux_wide.shape[0]
     above = pairs - 1 - z
-
-    def target(k):
-        return jnp.where(k < above, pairs - 1 - k, k - above)
-
-    def block_of(i):
-        t = target(i // 2)
-        return t * 2 + jnp.where(i % 2 == 0, 1 - h, h)
-
-    def load(i):
-        b = block_of(i)
+    last_sweep = ITERS - 1
+
+    def target(s, k):
+        line = jnp.where(k < above, pairs - 1 - k, k - above)
+        return jnp.where(s < last_sweep, (r + 1 + k) % rows_n, line)
+
+    def block_of(s, t, side):
+        return jnp.where(s < last_sweep, side * rows_n + t, t * 2 + side)
+
+    def piece_of(step):
+        return (r + rows_n - step) % rows_n
+
+    def load(step, i):
+        b, piece = block_of(0, target(0, i // 2), jnp.where(i % 2 == 0, 1 - h, h)), piece_of(step)
         return pltpu.make_async_copy(
-            kernel.at[pl.ds(pl.multiple_of(b * share_rows, share_rows), share_rows), :],
-            kernel_held.at[b], kernel_sem.at[i],
-        )
-
-    share_load = pltpu.make_async_copy(
-        boundary_start.at[pl.ds(pl.multiple_of(c * share_rows, share_rows), share_rows), :], share, share_sem
-    )
+            kernel.at[
+                pl.ds(pl.multiple_of(b * share_rows, share_rows), share_rows),
+                pl.ds(pl.multiple_of(piece * share_rows, share_rows), share_rows),
+            ],
+            kernel_held.at[b, piece], kernel_sem.at[step, i],
+        )
+
+    def start_rows(piece):
+        return boundary_start.at[pl.ds(pl.multiple_of((h * rows_n + piece) * share_rows, share_rows), share_rows), :]
+
+    def piece_load(piece):
+        return pltpu.make_async_copy(start_rows(piece), panels.at[0, piece], piece_sem.at[piece])
+
     volume_load = pltpu.make_async_copy(volume_start, volume, volume_sem)
     elem_load = pltpu.make_async_copy(elem_mats, elem_held, elem_sem)
-    share_load.start()
+
+    @pl.when(roots)
+    def _():
+        for piece in range(rows_n):
+            piece_load(piece).start()
+
     volume_load.start()
-    for i in range(cols_n):
-        load(i).start()
+    for step in range(rows_n):
+        for i in range(cols_n):
+            load(step, i).start()
     elem_load.start()
 
     barrier = pltpu.get_barrier_semaphore()
@@ -106,12 +123,13 @@
     @pl.when(moves)
     def _():
         greet(source_row, source_col)
+        greet(target_row, target_col)
 
     @pl.when((c == 0) & (r > 0))
     def _():
         greet(r - 1, cols_n - 1)
 
-    greeted = cols_n - 1 + rows_n - 1 + jnp.where(stays, 0, 1)
+    greeted = cols_n - 1 + rows_n - 1 + jnp.where(stays, 0, 2)
     greeted += jnp.where((c == cols_n - 1) & (r < rows_n - 1), 1, 0)
     pl.semaphore_wait(barrier, greeted)
 
@@ -121,31 +139,54 @@
             device_id=(row, col), device_id_type=pl.DeviceIdType.MESH,
         )
 
-    def move(par):
-        return remote(
-            share, panels.at[par, target_row], move_send, move_recv.at[par], target_row, target_col
+    def move_incident():
+        return remote(incident_own, incident, move_send.at[0], move_recv.at[0], target_row, target_col)
+
+    def move_diag():
+        return remote(diag_own, diag_row, move_send.at[1], move_recv.at[1], target_row, target_col)
+
+    def move_middle():
+        return remote(middle_out, middle, move_send.at[2], move_recv.at[2], source_row, source_col)
+
+    def start_copy(step):
+        piece = (r + step) % rows_n
+        return remote(
+            start_rows(piece), panels.at[0, piece], start_send.at[step - 1], start_recv, piece, c
         )
 
     def row_copy(par, step):
         piece = panels.at[par, r]
         return remote(
-            piece, piece, row_send.at[step - 1], row_recv.at[par, step - 1], (r + step) % rows_n, c
-        )
-
-    def pair_copy(par, t):
-        return remote(
-            partial.at[t * 2 + (1 - h)], from_pair.at[par, t], pair_send.at[t], pair_recv.at[par, t], r, partner
+            piece, piece, row_send.at[par, step - 1], row_recv.at[par, step - 1], (r + step) % rows_n, c
+        )
+
+    def row_sent(s, step):
+        return (s > 0) | ((r + step) % rows_n != z)
+
+    def pair_copy(par, s, t):
+        return remote(
+            partial.at[block_of(s, t, 1 - h)], from_pair.at[par, t], pair_send.at[t], pair_recv.at[par, t], r, partner
+        )
+
+    def turn_copy(par, t):
+        return remote(
+            partial.at[h * rows_n + t], from_row.at[par, r], turn_send.at[t], turn_recv.at[par, r], t, c
+        )
+
+    def turn_landed(par, t):
+        return remote(
+            partial.at[h * rows_n + t], from_row.at[par, t], turn_send.at[t], turn_recv.at[par, t], t, c
         )
 
     def up_copy(par, t):
         return remote(
-            partial.at[t * 2 + h], from_line.at[par, t + 1],
+            from_row.at[par, t], from_line.at[par, t + 1],
             line_send.at[t + 1], line_recv.at[par, t + 1], r, c + 2,
         )
 
     def down_copy(par, t):
         return remote(
-            partial.at[t * 2 + h], from_line.at[par, t], line_send.at[t], line_recv.at[par, t], r, c - 2
+            from_row.at[par, t], from_line.at[par, t], line_send.at[t], line_recv.at[par, t], r, c - 2
         )
 
     def flux_copy(par, piece, step):
@@ -198,62 +239,66 @@
         for step in range(1, rows_n):
             trace_copy(par, step).wait_send()
 
-    def relay_up(par, t):
-        up_copy(par, t).start()
-
-    def relay_down(par, t):
-        down_copy(par, t).start()
-
-    def take_piece(par, step, carry):
-        piece = (r + rows_n - step) % rows_n
-
-        @pl.when(step > 0)
+    def take_piece(s, par, step, carry):
+        piece = piece_of(step)
+        last_step = step == rows_n - 1
+
+        @pl.when((s == 0) & roots)
+        def _():
+            @pl.when(step > 0)
+            def _():
+                piece_load(piece).wait()
+
+        @pl.when((step > 0) & ((s > 0) | jnp.logical_not(roots)))
         def _():
             row_copy(par, jnp.maximum(step, 1)).wait_recv()
 
         wide = wide_of(panels[par, piece])
-        panel_wide[pl.ds(pl.multiple_of(piece * share_rows, share_rows), share_rows), :] = wide
-        place = lax.broadcasted_iota(jnp.int32, (cols_n * capacity, share_rows), 1)
-        picked = product(one_hot(place == flux_send[piece]), wide)
+        panel_wide[...] = wide
+        place = lax.broadcasted_iota(jnp.int32, (share_rows, cols_n * capacity), 0)
+        picked = lax.dot_general(
+            one_hot(place == flux_send[piece]), wide, (((0,), (0,)), ((), ())), preferred_element_type=jnp.float32
+        )
         picked = picked[:, :columns] + picked[:, columns:]
         flux_leaving[piece] = picked.reshape(cols_n, capacity, columns)
         for other in range(1, cols_n):
             flux_copy(par, piece, other).start()
         flux_landed[par, c, piece] = flux_leaving[piece, c]
-        return carry
-
-    def product_step(s, par, i, carry):
-        b = block_of(i)
-        t = target(i // 2)
-
-        @pl.when(s == 0)
-        def _():
-            load(i).wait()
-
-        high, low = parts(kernel_held[b])
-        place = lax.broadcasted_iota(jnp.int32, (share_rows, trace_wide.shape[1]), 0)
-        wide = product(high, panel_wide[...]) + product(low, panel_wide[...])
-        wide -= product(one_hot(place == trace_take[b]), trace_wide[b])
-        partial[b] = wide[:, :columns] + wide[:, columns:]
-
-        @pl.when(i % 2 == 0)
-        def _():
-            pair_copy(par, t).start()
-
-        @pl.when(i % 2 == 1)
-        def _():
-            pair_copy(par, t).wait_recv()
-            partial[b] += from_pair[par, t]
-
-            @pl.when((z == 0) & (t > z))
-            def _():
-                up_copy(par, t).start()
-
-            @pl.when((z == pairs - 1) & (t < z))
-            def _():
-                down_copy(par, t).start()
-
-        return carry
+
+        def product_step(i, carry):
+            t = target(s, i // 2)
+            theirs = i % 2 == 0
+            b = block_of(s, t, jnp.where(theirs, 1 - h, h))
+
+            @pl.when(s == 0)
+            def _():
+                load(step, i).wait()
+
+            high, low = parts(kernel_held[b, piece])
+            wide = product(high, panel_wide[...]) + product(low, panel_wide[...])
+            partial[b] += wide[:, :columns] + wide[:, columns:]
+
+            @pl.when(last_step & theirs)
+            def _():
+                pair_copy(par, s, t).start()
+
+            @pl.when(last_step & jnp.logical_not(theirs))
+            def _():
+                pair_copy(par, s, t).wait_recv()
+                stay = (s == last_sweep) | (t == r)
+
+                @pl.when(stay)
+                def _():
+                    from_row[par, t] = partial[b] + from_pair[par, t]
+
+                @pl.when(jnp.logical_not(stay))
+                def _():
+                    partial[b] += from_pair[par, t]
+                    turn_copy(par, t).start()
+
+            return carry
+
+        return lax.fori_loop(0, cols_n, product_step, carry)
 
     def volume_step_of(par, e, carry):
         nodes = pl.ds(pl.multiple_of(e * node_count, node_count), node_count)
@@ -264,99 +309,158 @@
         place = lax.broadcasted_iota(jnp.int32, (node_count, slots), 0) + e * node_count
         wide -= product(one_hot(place == flux_take[...]), flux_wide[...])
         volume[nodes, :] = field - volume_step * (field + wide[:, :columns] + wide[:, columns:])
-        node = lax.broadcasted_iota(jnp.int32, (face_count, face_count), 1)
-        face = product(one_hot(node == face_rows[e]), wide_of(faces[par, e]))
+        node = lax.broadcasted_iota(jnp.int32, (face_count, face_count), 0)
+        face = lax.dot_general(
+            one_hot(node == face_rows[e]), wide_of(faces[par, e]), (((0,), (0,)), ((), ())),
+            preferred_element_type=jnp.float32,
+        )
         matched = face[:, :columns] + face[:, columns:]
         lower = pl.ds(pl.multiple_of(e * node_count, node_count), face_count)
         volume[lower, :] += volume_step * face_weight * matched
         return carry
 
-    gaps = max(1, pairs - 2)
+    gaps = pairs - 1
     chunk = -(-elem_count // gaps)
 
-    def relay_step(par, stage, carry):
-        @pl.when((z >= 1) & (z <= stage) & (stage <= pairs - 2))
+    def wait_turn(s, par, t):
+        @pl.when((s < last_sweep) & (t != r))
+        def _():
+            turn_landed(par, t).wait_recv()
+
+    def relay_step(s, par, stage, carry):
+        @pl.when(z <= stage)
         def _():
             t = pairs - 1 + z - stage
-            up_copy(par, t - 0).wait_recv()
-            partial[t * 2 + h] += from_line[par, t + 1]
+            wait_turn(s, par, t)
+
+            @pl.when(z > 0)
+            def _():
+                up_copy(par, t).wait_recv()
+                from_row[par, t] += from_line[par, t + 1]
+
             up_copy(par, t).start()
 
-        @pl.when((z <= pairs - 2) & (above <= stage) & (stage <= pairs - 2))
+        @pl.when(above <= stage)
         def _():
             t = stage - above
-            down_copy(par, t).wait_recv()
-            partial[t * 2 + h] += from_line[par, t]
+            wait_turn(s, par, t)
+
+            @pl.when(above > 0)
+            def _():
+                down_copy(par, t).wait_recv()
+                from_row[par, t] += from_line[par, t]
+
             down_copy(par, t).start()
 
-        first = jnp.minimum((stage - 1) * chunk, elem_count)
-        last = jnp.minimum(stage * chunk, elem_count)
+        @pl.when(stage == 0)
+        def _():
+            @pl.when(s == 0)
+            def _():
+                elem_load.wait()
+
+            for piece in range(rows_n):
+                for other in range(1, cols_n):
+                    flux_copy(par, piece, other).wait_recv()
+            flux_wide[...] = wide_of(flux_landed[par].reshape(slots, columns))
+
+            @pl.when(has_prev)
+            def _():
+                for e in range(elem_count):
+                    face_copy(par, e).wait_recv()
+
+            wait_faces_sent(par)
+            wait_traces_sent(par)
+
+        first = jnp.minimum(stage * chunk, elem_count)
+        last = jnp.minimum((stage + 1) * chunk, elem_count)
         lax.fori_loop(first, last, functools.partial(volume_step_of, par), 0)
         return carry
 
+    def take_trace(b, carry):
+        place = lax.broadcasted_iota(jnp.int32, (share_rows, trace_wide.shape[1]), 0)
+        wide = product(one_hot(place == trace_take[b]), trace_wide[b])
+        partial[b] = -(wide[:, :columns] + wide[:, columns:])
+        return carry
+
     def sweep(s, carry):
         par = s % 2
-        lax.fori_loop(0, rows_n, functools.partial(take_piece, par), 0)
-
         for step in range(1, rows_n):
             trace_copy(par, step).wait_recv()
         for b in range(cols_n):
             landed = trace_landed[par, :, b].reshape(rows_n * capacity, columns)
             trace_wide[b] = wide_of(landed)
-
-        lax.fori_loop(0, cols_n, functools.partial(product_step, s, par), 0)
-
-        @pl.when(s == 0)
-        def _():
-            elem_load.wait()
-
-        for piece in range(rows_n):
-            for other in range(1, cols_n):
-                flux_copy(par, piece, other).wait_recv()
-        flux_wide[...] = wide_of(flux_landed[par].reshape(slots, columns))
-
-        @pl.when(has_prev)
-        def _():
-            for e in range(elem_count):
-                face_copy(par, e).wait_recv()
-
-        wait_faces_sent(par)
-        wait_traces_sent(par)
-        lax.fori_loop(1, 1 + gaps, functools.partial(relay_step, par), 0)
-
-        @pl.when(s < ITERS - 1)
+        lax.fori_loop(0, cols_n, take_trace, 0)
+
+        def middle_of():
+            held = panels[par, r]
+            return held - boundary_step * (diag[...] * held - incident[...])
+
+        @pl.when((s == last_sweep) & moves)
+        def _():
+            middle_out[...] = middle_of()
+            move_middle().start()
+
+        @pl.when((s == last_sweep) & stays)
+        def _():
+            middle[...] = middle_of()
+
+        lax.fori_loop(0, rows_n, functools.partial(take_piece, s, par), 0)
+        lax.fori_loop(0, gaps, functools.partial(relay_step, s, par), 0)
+
+        @pl.when(s < last_sweep)
         def _():
             send_faces(1 - par)
             send_traces(1 - par)
 
-        own = z * 2 + h
+        @pl.when((s == 0) & moves)
+        def _():
+            move_diag().wait_recv()
+            move_incident().wait_recv()
+
+        @pl.when(s == 0)
+        def _():
+            diag[...] = jnp.broadcast_to(diag_row[...], (columns, share_rows)).T
+
+        @pl.when((s == last_sweep) & moves)
+        def _():
+            move_middle().wait_recv()
+
+        wait_turn(s, par, z)
 
         @pl.when(z > 0)
         def _():
             up_copy(par, z).wait_recv()
-            partial[own] += from_line[par, z + 1]
-
-        @pl.when(z < pairs - 1)
+            from_row[par, z] += from_line[par, z + 1]
+
+        @pl.when(above > 0)
         def _():
             down_copy(par, z).wait_recv()
-            partial[own] += from_line[par, z]
-
-        @pl.when(moves)
-        def _():
-            move(par).wait_send()
-
-        held = share[...]
-        middle = held - boundary_step * (diag[...] * held - incident[...])
-        share[...] = middle - boundary_step * partial[own]
-
-        @pl.when((s < ITERS - 1) & moves)
-        def _():
-            move(1 - par).start()
-
+            from_row[par, z] += from_line[par, z]
+
+        @pl.when(s == last_sweep)
+        def _():
+            panels[1 - par, r] = middle[...] - boundary_step * from_row[par, z]
+
+        @pl.when(s < last_sweep)
+        def _():
+            panels[1 - par, r] = middle_of() - boundary_step * from_row[par, z]
+            for step in range(1, rows_n):
+                row_copy(1 - par, step).start()
+
+        return carry
+
+    def drain(s, par):
         for step in range(1, rows_n):
-            row_copy(par, step).wait_send()
+            @pl.when(row_sent(s, step))
+            def _():
+                row_copy(par, step).wait_send()
+
         for t in range(pairs):
-            pair_copy(par, t).wait_send()
+            pair_copy(par, s, t).wait_send()
+
+            @pl.when((s < last_sweep) & (t != r))
+            def _():
+                turn_copy(par, t).wait_send()
 
             @pl.when(t > z)
             def _():
@@ -370,29 +474,20 @@
             for other in range(1, cols_n):
                 flux_copy(par, piece, other).wait_send()
 
-        @pl.when(s < ITERS - 1)
-        def _():
-            finish_spread(1 - par)
-
-        return carry
-
-    def finish_spread(par):
-        @pl.when(stays)
-        def _():
-            panels[par, r] = share[...]
-
-        @pl.when(moves)
-        def _():
-            move(par).wait_recv()
-
+    @pl.when(roots)
+    def _():
         for step in range(1, rows_n):
-            row_copy(par, step).start()
-
-    share_load.wait()
+            start_copy(step).start()
 
     @pl.when(moves)
     def _():
-        move(0).start()
+        move_diag().start()
+        move_incident().start()
+
+    @pl.when(stays)
+    def _():
+        diag_row[...] = diag_own[...]
+        incident[...] = incident_own[...]
 
     @pl.when(jnp.logical_not(has_prev))
     def _():
@@ -401,8 +496,27 @@
     volume_load.wait()
     send_faces(0)
     send_traces(0)
-    finish_spread(0)
-    lax.fori_loop(0, ITERS, sweep, 0)
+
+    @pl.when(roots)
+    def _():
+        piece_load(r).wait()
+
+    @pl.when(jnp.logical_not(roots))
+    def _():
+        remote(start_rows(r), panels.at[0, r], start_send.at[0], start_recv, z, c).wait_recv()
+
+    for step in range(1, rows_n):
+        @pl.when(row_sent(0, step))
+        def _():
+            row_copy(0, step).start()
+
+    def sweep_and_drain(s, carry):
+        sweep(s, carry)
+        drain(s, s % 2)
+        return carry
+
+    lax.fori_loop(0, ITERS, sweep_and_drain, 0)
+    share = panels.at[ITERS % 2, r]
 
     keep = pltpu.make_async_copy(share, out.at[c], out_sem)
     keep.start()
@@ -466,13 +580,23 @@
         def _():
             final_down(share, c, step).wait_send()
 
+    @pl.when(roots)
+    def _():
+        for step in range(1, rows_n):
+            start_copy(step).wait_send()
+
+    @pl.when(moves)
+    def _():
+        move_diag().wait_send()
+        move_incident().wait_send()
+        move_middle().wait_send()
+
 
 def sweeps(boundary_start, volume_flat, kernel, elem_mats, diag, incident, plans, capacity, face_rows):
     rows_n, cols_n = lax.axis_size("row"), lax.axis_size("col")
     pairs = cols_n // 2
     share_rows, columns = incident.shape
-    panel_rows = kernel.shape[1]
-    elem_count, face_count = face_rows.shape[:2]
+    elem_count, _, face_count = face_rows.shape
     block = (share_rows, columns)
     slots = rows_n * cols_n * capacity
     f32, bf16 = jnp.float32, jnp.bfloat16
@@ -480,13 +604,18 @@
     in_smem = pl.BlockSpec(memory_space=pltpu.SMEM)
     dma = pltpu.SemaphoreType.DMA
     scratch = [
-        pltpu.VMEM((cols_n, share_rows, panel_rows), f32),
+        pltpu.VMEM((cols_n, rows_n, share_rows, share_rows), f32),
         pltpu.VMEM(elem_mats.shape, f32),
+        pltpu.VMEM((1, share_rows), f32),
+        pltpu.VMEM(block, f32),
+        pltpu.VMEM(block, f32),
+        pltpu.VMEM(block, f32),
         pltpu.VMEM(block, f32),
         pltpu.VMEM((2, rows_n) + block, f32),
-        pltpu.VMEM((panel_rows, 2 * columns), bf16),
+        pltpu.VMEM((share_rows, 2 * columns), bf16),
         pltpu.VMEM((cols_n,) + block, f32),
         pltpu.VMEM((2, pairs) + block, f32),
+        pltpu.VMEM((2, rows_n) + block, f32),
         pltpu.VMEM((2, pairs + 1) + block, f32),
         pltpu.VMEM((rows_n, cols_n, capacity, columns), f32),
         pltpu.VMEM((2, cols_n, rows_n, capacity, columns), f32),
@@ -495,9 +624,9 @@
         pltpu.VMEM((2, rows_n, cols_n, capacity, columns), f32),
         pltpu.VMEM((cols_n, rows_n * capacity, 2 * columns), bf16),
         pltpu.VMEM((2, elem_count, face_count, columns), f32),
-        dma((cols_n,)), dma, dma, dma,
-        dma, dma((2,)), dma((rows_n - 1,)), dma((2, rows_n - 1)),
-        dma((pairs,)), dma((2, pairs)), dma((pairs + 1,)), dma((2, pairs + 1)),
+        dma((rows_n, cols_n)), dma, dma, dma((rows_n,)),
+        dma((3,)), dma((3,)), dma((rows_n - 1,)), dma, dma((2, rows_n - 1)), dma((2, rows_n - 1)),
+        dma((pairs,)), dma((2, pairs)), dma((rows_n,)), dma((2, rows_n)), dma((pairs + 1,)), dma((2, pairs + 1)),
         dma((rows_n, cols_n - 1)), dma((2, rows_n, cols_n - 1)),
         dma((rows_n - 1,)), dma((2, rows_n - 1)),
         dma((elem_count,)), dma((2, elem_count)),
@@ -566,12 +695,12 @@
     plans = (
         jnp.maximum(plan[0], 0),
         plan[1].reshape(cols_n, 1, rows_n * capacity),
-        plan[2].reshape(rows_n, cols_n * capacity, 1),
+        plan[2].reshape(rows_n, 1, cols_n * capacity),
         plan[3].reshape(1, devices * capacity),
     )
     volume_final, boundary_final = sweeps(
         boundary_start, volume_start.reshape(elem_count * node_count, columns), kernel, elem_mats,
-        diag_part[:, None], incident, plans, capacity, face_match[:, :, None],
+        diag_part[None, :], incident, plans, capacity, face_match[:, None, :],
     )
     return (
         boundary_final.reshape(boundary_start.shape),

time: 226 us -> 234 us (1.035)
  Pallas kernels: 204 us -> 215 us
  local copies, waits for them, and re-layouts: 15 us -> 11.3 us
    pallas_call x1, Pallas kernels: 204 us -> 215 us  [sweeps(): pl.pallas_call(sweeps_kernel, out_shape=[jax.ShapeDtypeStruct(volume_flat...]
    broadcast_in_dim x2 -> x0, local copies, waits for them, and re-layouts: 3.06 us -> none  [the longest x1 1.53 us: shards(): diag_part[:, None]]
where the time goes in v2:
time: 234 us; the launch traced here: 233 us
  Pallas kernels  215 us (92%)
  local copies, waits for them, and re-layouts  11.3 us (5%)
  other arithmetic  5.78 us (2%)
    pallas_call x1, Pallas kernels, sweeps(): pl.pallas_call(sweeps_kernel, out_shape=[jax.ShapeDtypeStruct(volume_flat...  215 us
    unnamed x3, local copies, waits for them, and re-layouts  6.62 us

profile of v2, /device:TPU:0, one launch (start us, length us, event | category | flops | bytes accessed | tf_op | source)
XLA Modules:
  0.0 233.4 jit_solution(11892900288237481151)
XLA Ops:
  0.7 0.1 eq.74
  0.8 0.1 eq.68
  0.9 0.5 broadcast.50
  1.4 1.6 reduce.7
  3.1 1.6 reduce.6
  4.8 0.1 bitcast_compare_fusion
  4.9 0.9 concatenate.15
  5.8 0.9 concatenate.16
  6.7 0.3 convolution_select_fusion
  7.0 2.3 select_reduce_fusion
  9.4 0.7 slice.22.refs_9_
  10.0 0.7 reshape_squeeze.15.refs_8_
  10.7 0.7 reshape_squeeze.14.refs_7_
  11.4 0.7 max.10.refs_6_
  12.0 215.3 %shard_map.122 = (f32[4096,128]{1,0:T(8,128)}, f32[8,512,128]{2,1,0:T(8,128)}) custom-call(f32[4096,128]{1,0:T(8,128)} %refs_0_.1, f32[4096,128]{1,0:T(8,128)} %bitcast.9, f32[4096,2048]{1,0:T(8,128)} %refs_2_.1, f32[8,512,512]{2,1,0:T(8,128)} %refs_3_.1, f32[1,512]{1,0:T(1,128)} %bitcast.13, f32[512,128]{1,0:T(8,128)} %refs_5_.1, s32[1024]{0:T(1024)} %max.10.refs_6_, ...), custom_call_target="tpu_custom_call" | custom-call | flops 1000 | bytes 150000000 | tf_op jit(solution)/shard_map/pallas_call | solution.py:635
  227.3 3.0 %copy.27 = f32[4096,128]{1,0:T(8,128)} copy(f32[4096,128]{1,0:T(8,128)} %bitcast.11) | data formatting | bytes 4194304
  230.3 3.1 %copy.28 = f32[8,512,128]{2,1,0:T(8,128)} copy(f32[8,512,128]{2,1,0:T(8,128)} %bitcast.10) | data formatting | bytes 4194304
  (17 shorter events, 0.2 us)
